TPU v7x, 128 devices: a whole 4x4x4 slice. The times are simulated.
128 devices in a mesh: rows: 32 (over x, z, core), units: 4 (over y).
Axes of the slice: x: 4, y: 4, z: 4, core: 2. Of those that a mesh axis runs over, the one named last changes fastest.
Arguments:
- residuals: bfloat16 [524288, 2048], P(('rows', 'units')), may hold values from -24 to 24
- loadings: bfloat16 [524288, 256], P(('rows', 'units')), may hold values from -6 to 6
- zero_points: bfloat16 [1024, 2048], P('units'), may hold values from -0.375 to 0.375
- sketch_matrix: bfloat16 [2048, 256], replicated, may hold values from -0.125 to 0.125
- use_lists: int32 [4096, 4], P(('rows', 'units')), may hold values from 0 to 15, all different within a row
Outputs:
- star_basis: float32 [524288, 256], P(('rows', 'units'))
- bin_modes: float32 [2048, 256], P(('rows', 'units'))
Inputs may be any that keep to these rules, and one draw needn't show every extreme that they name: `use_lists`: each row names 4 different groups; every group is named by some row.
All inputs are finite; a program needn't handle non-finite values.
Results may differ from a plain program's by a relative error of at most 0.003.
Values may be sent and summed in bfloat16 or wider, within the bound.
No kernel may reach another device: no remote copies, remote signals or barrier semaphores. Data moves between devices by JAX's collectives and lax.ppermute only.
A program may use at most 192 MiB of HBM per device.

v0:
```python
import jax
import jax.numpy as jnp
from jax import lax
from jax.sharding import PartitionSpec as P

GROUP = 64
USES = 4
BLOCK_STARS = 128


def on_device(residuals, loadings, zero_points, sketch_matrix, use_lists):
    gathered = lax.all_gather(zero_points, "units", axis=0, tiled=True)
    local_rows, width_bins = residuals.shape
    group_count = gathered.shape[0] // GROUP
    block_count = use_lists.shape[0]
    tables = gathered.reshape(group_count, GROUP, width_bins)
    chosen = tables[use_lists].reshape(block_count, USES * GROUP, width_bins)
    offsets = jnp.einsum(
        "bsk,bkn->bsn",
        loadings.reshape(block_count, BLOCK_STARS, USES * GROUP),
        chosen,
        preferred_element_type=jnp.float32,
    )
    corrected = (
        residuals.reshape(block_count, BLOCK_STARS, width_bins).astype(jnp.float32) - offsets
    ).astype(jnp.bfloat16)
    corrected = corrected.reshape(local_rows, width_bins)
    sketched = jnp.dot(corrected, sketch_matrix, preferred_element_type=jnp.float32)
    sketch_low = sketched.astype(jnp.bfloat16)
    devices_all = lax.axis_size(("rows", "units"))
    total_stars = local_rows * devices_all
    gram_local = jnp.dot(sketched.T, sketched, precision=lax.Precision.HIGHEST) / total_stars
    lower_factor = jnp.linalg.cholesky(lax.psum(gram_local, ("rows", "units")))
    star_basis = lax.linalg.triangular_solve(
        lower_factor, sketched, left_side=False, lower=True, transpose_a=True
    )
    bin_share = width_bins // devices_all
    full_terms = jnp.einsum("sn,sm->nm", corrected, sketch_low, preferred_element_type=jnp.float32)
    summed_all = lax.psum(full_terms, ("rows", "units"))
    first_bin = lax.axis_index(("rows", "units")) * bin_share
    summed = lax.dynamic_slice_in_dim(summed_all, first_bin, bin_share, 0)
    raw_modes = summed / total_stars
    bin_modes = lax.linalg.triangular_solve(
        lower_factor, raw_modes, left_side=False, lower=True, transpose_a=True
    )
    return (star_basis, bin_modes)


def solution(mesh):
    in_specs = (
        P(("rows", "units"), None),
        P(("rows", "units"), None),
        P("units", None),
        P(),
        P(("rows", "units"), None),
    )
    out_specs = (P(("rows", "units"), None), P(("rows", "units"), None))
    return jax.shard_map(
        on_device, mesh=mesh, in_specs=in_specs, out_specs=out_specs, check_vma=False
    )
```

profile of v0, /device:TPU:1, one launch (start us, length us, event | category | flops | bytes accessed | tf_op | source)
XLA Modules:
  0.0 364.4 jit_solution(14588423251606039512)
XLA Ops:
  7.2 0.0 copy-start
  7.2 0.0 all-gather.2.cloned.1.call-start
  7.2 0.7 all-gather.2.cloned.1.call-update
  7.9 0.0 all-reduce.4.cloned.1.call-start
  8.0 0.7 compare_select_fusion
  8.6 0.1 copy.11
  8.7 0.1 reshape.66
  8.9 52.1 %all-gather.2.cloned.1.call-done = bf16[1024,2048]{1,0:T(8,128)(2,1)} async-done(((bf16[256,2048]{1,0:T(8,128)(2,1)}), bf16[1024,2048]{1,0:T(8,128)(2,1)}) %all-gather.2.cloned.1.call-update) | async-done | bytes 4194320 | tf_op jit(solution)/shard_map/all_gather | solution.py:12
  60.9 14.9 %gather_fusion = bf16[128,64,2048]{2,1,0:T(8,128)(2,1)} fusion(bf16[16,64,2048]{2,1,0:T(8,128)(2,1)} %bitcast.51, s32[1024]{0:T(1024)S(1)} %pad_clamp_fusion), kind=kCustom, calls=%fused_computation | custom fusion | bytes 67109376 | tf_op jit(solution)/shard_map/gather | solution.py:17
  75.8 0.0 copy-done
  75.8 23.4 %fusion = bf16[32,128,2048]{2,1,0:T(8,128)(2,1)} fusion(bf16[32,128,2048]{2,1,0:T(8,128)(2,1)} %bitcast.53, bf16[32,128,256]{2,1,0:T(8,128)(2,1)S(1)} %bitcast.50, bf16[32,256,2048]{2,1,0:T(8,128)(2,1)} %bitcast.52), kind=kOutput, calls=%fused_computation.4 | convolution fusion | flops 4320133120 | bytes 69206016 | tf_op jit(solution)/shard_map/bsk,bkn->bsn/dot_general | solution.py:18
  99.2 0.0 copy-done.5
  99.3 10.3 %fusion.16 = f32[4096,256]{1,0:T(8,128)S(1)} fusion(bf16[4096,2048]{1,0:T(8,128)(2,1)} %bitcast.54, bf16[2048,256]{1,0:T(8,128)(2,1)S(1)} %copy-done.5), kind=kOutput, calls=%fused_computation.44 | convolution fusion | flops 4294967296 | bytes 22020096 | tf_op jit(solution)/shard_map/dot_general | solution.py:28
  109.6 0.2 copy-done.4
  109.8 6.3 %fusion.3 = f32[2048,256]{1,0:T(8,128)} fusion(bf16[4096,2048]{1,0:T(8,128)(2,1)S(1)} %bitcast.55, f32[4096,256]{1,0:T(8,128)S(1)} %fusion.16), kind=kOutput, calls=%fused_computation.9 | convolution fusion | flops 4296015872 | bytes 23068672 | tf_op jit(solution)/shard_map/sn,sm->nm/dot_general | solution.py:38
  116.1 0.0 copy-done.2
  116.1 7.4 %convolution_multiply_fusion = f32[256,256]{0,1:T(8,128)} fusion(f32[4096,256]{1,0:T(8,128)S(1)} %fusion.16), kind=kOutput, calls=%fused_computation.11 | convolution fusion | flops 3221291008 | bytes 4456448 | tf_op jit(solution)/shard_map/dot_general | solution.py:32
  123.6 0.0 all-reduce.4.cloned.1.call-update
  123.6 152.5 %all-reduce.4.cloned.1.call-done = (f32[256,256]{0,1:T(8,128)}, f32[2048,256]{1,0:T(8,128)}) async-done(((f32[256,256]{0,1:T(8,128)}, f32[2048,256]{1,0:T(8,128)}), (f32[256,256]{0,1:T(8,128)}, f32[2048,256]{1,0:T(8,128)})) %all-reduce.4.cloned.1.call-update) | async-done | bytes 2359312 | tf_op jit(solution)/shard_map/psum | solution.py:33
  276.1 1.2 copy.13
  277.4 1.0 fusion.5
  278.4 11.7 %cholesky.50 = f32[128,128]{1,0:T(8,128)S(1)} custom-call(f32[128,128]{1,0:T(8,128)S(1)} %cholesky.118), custom_call_target="Cholesky" | custom-call | tf_op jit(solution)/shard_map/jit(cholesky)/cholesky | solution.py:33
  290.1 9.8 %custom-call.16 = f32[1,128,128]{1,2,0:T(8,128)S(1)} custom-call(f32[1,128,128]{2,1,0:T(8,128)S(1)} %get-tuple-element.29), custom_call_target="InvertDiagBlocksLowerTriangular" | custom-call | tf_op jit(solution)/shard_map/jit(cholesky)/cholesky | solution.py:33
  300.0 0.2 constant_dynamic-update-slice_fusion.1
  300.2 0.3 convolution_subtract_fusion.1
  300.5 11.7 %cholesky.105 = f32[128,128]{1,0:T(8,128)S(1)} custom-call(f32[128,128]{1,0:T(8,128)S(1)} %convolution_subtract_fusion.1), custom_call_target="Cholesky" | custom-call | tf_op jit(solution)/shard_map/jit(cholesky)/cholesky | solution.py:33
  312.2 0.7 compare_reduce_fusion
  314.2 0.1 triangular_solve.73
  314.3 3.9 %while.1 = (s32[]{:T(128)}, f32[256,256]{1,0:T(8,128)S(1)}, s32[2,2]{1,0:T(2,128)S(1)}, f32[2,128,128]{2,1,0:T(8,128)S(1)}, s32[]{:T(128)}) while((s32[]{:T(128)}, f32[256,256]{1,0:T(8,128)S(1)}, s32[2,2]{1,0:T(2,128)S(1)}, f32[2,128,128]{2,1,0:T(8,128)S(1)}, s32[]{:T(128)}) %tuple.29), condition=%wide.while_cond, body=%wide.while_body.sunk | while | flops 2 | bytes 131181 | solution.py:34
  314.3 0.6 fusion.31
  314.9 1.3 bitcast_dynamic-update-slice_fusion.2
  316.2 0.6 fusion.31
  316.8 1.3 bitcast_dynamic-update-slice_fusion.2
  318.1 19.9 %custom-call.17 = f32[2,128,128]{1,2,0:T(8,128)S(1)} custom-call(f32[2,128,128]{2,1,0:T(8,128)S(1)} %get-tuple-element.9), custom_call_target="InvertDiagBlocksLowerTriangular" | custom-call | tf_op jit(solution)/shard_map/triangular_solve | solution.py:34
  338.0 0.0 copy-start.3
  338.1 3.7 %fusion.1 = f32[4096,128]{0,1:T(8,128)S(1)} fusion(f32[4096,256]{1,0:T(8,128)} %copy-done.2, f32[2,128,128]{1,2,0:T(8,128)S(1)} %custom-call.17), kind=kOutput, calls=%fused_computation.7 | convolution fusion | flops 805306368 | bytes 4259840 | tf_op jit(solution)/shard_map/triangular_solve | solution.py:34
  341.8 0.7 dynamic-slice_multiply_fusion
  342.5 0.2 fusion.9
  342.7 0.2 convolution_subtract_fusion.2
  342.9 0.2 fusion.10
  343.1 0.6 pad_maximum_fusion.1
  343.7 0.0 copy-done.3
  343.7 3.6 convolution_subtract_fusion
  347.3 2.0 fusion.11
  349.3 0.0 copy-start.1
  349.3 2.4 pad_maximum_fusion
  351.7 5.6 %copy.14 = f32[4096,256]{1,0:T(8,128)} copy(f32[4096,256]{0,1:T(8,128)} %pad_maximum_fusion) | data formatting | bytes 8388608
  357.3 0.0 copy-done.1
  (13 shorter events, 0.2 us)
Async XLA Ops:
  7.2 68.7 %copy-start = (bf16[4096,256]{1,0:T(8,128)(2,1)S(1)}, bf16[4096,256]{1,0:T(8,128)(2,1)}, u32[]{:S(2)}) copy-start(bf16[4096,256]{1,0:T(8,128)(2,1)} %param.6) | copy-start | bytes 6291460
  7.2 53.8 %all-gather.2.cloned.1.call-start = ((), (), s32[]{:S(2)}) async-start(), calls=%async_computation | async-start | bytes 5242880 | tf_op jit(solution)/shard_map/all_gather | solution.py:12
  7.9 268.2 %all-reduce.4.cloned.1.call-start = ((), (), s32[]{:S(2)}) async-start(), calls=%async_computation.1 | async-start | bytes 4718592 | tf_op jit(solution)/shard_map/psum | solution.py:33
  75.8 23.4 %copy-start.5 = (bf16[2048,256]{1,0:T(8,128)(2,1)S(1)}, bf16[2048,256]{1,0:T(8,128)(2,1)}, u32[]{:S(2)}) copy-start(bf16[2048,256]{1,0:T(8,128)(2,1)} %param.8) | copy-start | bytes 3145732
  99.3 10.5 %copy-start.4 = (bf16[32,128,2048]{2,1,0:T(8,128)(2,1)S(1)}, bf16[32,128,2048]{2,1,0:T(8,128)(2,1)}, u32[]{:S(2)}) copy-start(bf16[32,128,2048]{2,1,0:T(8,128)(2,1)} %fusion) | copy-start | bytes 50331652
  109.8 6.3 %copy-start.2 = (f32[4096,256]{1,0:T(8,128)}, f32[4096,256]{1,0:T(8,128)S(1)}, u32[]{:S(2)}) copy-start(f32[4096,256]{1,0:T(8,128)S(1)} %fusion.16) | copy-start | bytes 12582916
  338.0 5.7 %copy-start.3 = (f32[4096,256]{1,0:T(8,128)S(1)}, f32[4096,256]{1,0:T(8,128)}, u32[]{:S(2)}) copy-start(f32[4096,256]{1,0:T(8,128)} %copy-done.2) | copy-start | bytes 12582916
  349.3 8.0 %copy-start.1 = (bf16[4096,256]{1,0:T(8,128)(2,1)S(1)}, bf16[4096,256]{1,0:T(8,128)(2,1)}, u32[]{:S(2)}) copy-start(bf16[4096,256]{1,0:T(8,128)(2,1)} %param.6) | copy-start | bytes 6291460
Sparse Core Ops, SparseCore 0:
  9.7 51.2 all-gather.1
  123.7 152.3 all-reduce.3
where the time goes:
time: 369 us; the launch traced here: 364 us
  waiting for transfers between devices  205 us (56%)
  other arithmetic  59.4 us (16%)
  matrix products  57.9 us (16%)
  local copies, waits for them, and re-layouts  26.1 us (7%)
  between operations  15.7 us (4%)
    psum x1, waiting for transfers between devices, on_device(): lower_factor = jnp.linalg.cholesky(lax.psum(gram_local, ('rows', 'units')))  153 us
    all_gather x1, waiting for transfers between devices, on_device(): gathered = lax.all_gather(zero_points, 'units', axis=0, tiled=True)  52.1 us
    another operation x6, other arithmetic, on_device(): lower_factor = jnp.linalg.cholesky(lax.psum(gram_local, ('rows', 'units')))  34 us
    dot_general x1, matrix products, on_device(): jnp.einsum('bsk,bkn->bsn', loadings.reshape(block_count, BLOCK_STARS, USE...  23.4 us
    another operation x4, other arithmetic, on_device(): lax.linalg.triangular_solve(lower_factor, sketched, left_side=False, lowe...  22.3 us
    gather x1, local copies, waits for them, and re-layouts, on_device(): chosen = tables[use_lists].reshape(block_count, USES * GROUP, width_bins)  14.9 us
    dot_general x1, matrix products, on_device(): jnp.dot(corrected, sketch_matrix, preferred_element_type=jnp.float32)  10.3 us
    another operation x3, matrix products, on_device(): lax.linalg.triangular_solve(lower_factor, sketched, left_side=False, lowe...  9.32 us
  transfers between devices with their start and end apart: 2, of which 2 were waited for; matrix products, arithmetic and copies ran while one was open for 0% of the time, Pallas kernels for 0%

commit v1 on v0

--- a/solution.py
+++ b/solution.py
@@ -30,7 +30,7 @@
     devices_all = lax.axis_size(("rows", "units"))
     total_stars = local_rows * devices_all
     gram_local = jnp.dot(sketched.T, sketched, precision=lax.Precision.HIGHEST) / total_stars
-    lower_factor = jnp.linalg.cholesky(lax.psum(gram_local, ("rows", "units")))
+    lower_factor = jnp.linalg.cholesky(lax.psum(lax.psum(gram_local, "rows"), "units"))
     star_basis = lax.linalg.triangular_solve(
         lower_factor, sketched, left_side=False, lower=True, transpose_a=True
     )

time: 369 us -> 438 us (1.19)
  waiting for transfers between devices: 205 us -> 263 us
  matrix products: 57.9 us -> 63.1 us
    psum x1 -> x3, waiting for transfers between devices: 153 us -> 211 us  [the longest x1 103 us: on_device(): lax.psum(gram_local, 'rows')]
    dot_general x1, matrix products: 6.31 us -> 13.2 us  [on_device(): jnp.einsum('sn,sm->nm', corrected, sketch_low, preferred_element_type=jnp...]
  transfers between devices with their start and end apart: 2 -> 4, of which waited for: 2 -> 4; matrix products, arithmetic and copies ran while one was open for 0% -> 21% of each run, Pallas kernels for 0% -> 0%
where the time goes in v1:
time: 438 us; the launch traced here: 430 us
  waiting for transfers between devices  263 us (60%)
  matrix products  63.1 us (14%)
  other arithmetic  59.4 us (14%)
  local copies, waits for them, and re-layouts  27.9 us (6%)
  between operations  15.6 us (4%)
    psum x1, waiting for transfers between devices, on_device(): lax.psum(gram_local, 'rows')  103 us
    psum x1, waiting for transfers between devices, on_device(): summed_all = lax.psum(full_terms, ('rows', 'units'))  79.4 us
    all_gather x1, waiting for transfers between devices, on_device(): gathered = lax.all_gather(zero_points, 'units', axis=0, tiled=True)  52.1 us
    another operation x6, other arithmetic, on_device(): jnp.linalg.cholesky(lax.psum(lax.psum(gram_local, 'rows'), 'units'))  34.2 us
    psum x1, waiting for transfers between devices, on_device(): lax.psum(lax.psum(gram_local, 'rows'), 'units')  28.1 us
    dot_general x1, matrix products, on_device(): jnp.einsum('bsk,bkn->bsn', loadings.reshape(block_count, BLOCK_STARS, USE...  23.4 us
    another operation x4, other arithmetic, on_device(): lax.linalg.triangular_solve(lower_factor, sketched, left_side=False, lowe...  22.1 us
    gather x1, local copies, waits for them, and re-layouts, on_device(): chosen = tables[use_lists].reshape(block_count, USES * GROUP, width_bins)  14.9 us
  transfers between devices with their start and end apart: 4, of which 4 were waited for; matrix products, arithmetic and copies ran while one was open for 21% of the time, Pallas kernels for 0%

profile of v1, /device:TPU:1, one launch (start us, length us, event | category | flops | bytes accessed | tf_op | source)
XLA Modules:
  0.0 429.6 jit_solution(16348853287514028164)
XLA Ops:
  7.2 0.0 copy-start
  7.2 0.0 all-gather.2.cloned.1.call-start
  7.2 0.7 all-gather.2.cloned.1.call-update
  7.9 0.0 all-reduce.5.cloned.1.call-start
  8.0 0.7 compare_select_fusion
  8.6 0.1 copy.11
  8.7 0.1 reshape.66
  8.9 52.1 %all-gather.2.cloned.1.call-done = bf16[1024,2048]{1,0:T(8,128)(2,1)} async-done(((bf16[256,2048]{1,0:T(8,128)(2,1)}), bf16[1024,2048]{1,0:T(8,128)(2,1)}) %all-gather.2.cloned.1.call-update) | async-done | bytes 4194320 | tf_op jit(solution)/shard_map/all_gather | solution.py:12
  60.9 14.9 %gather_fusion = bf16[128,64,2048]{2,1,0:T(8,128)(2,1)} fusion(bf16[16,64,2048]{2,1,0:T(8,128)(2,1)} %bitcast.51, s32[1024]{0:T(1024)S(1)} %pad_clamp_fusion), kind=kCustom, calls=%fused_computation | custom fusion | bytes 67109376 | tf_op jit(solution)/shard_map/gather | solution.py:17
  75.8 23.4 %fusion = bf16[32,128,2048]{2,1,0:T(8,128)(2,1)} fusion(bf16[32,128,2048]{2,1,0:T(8,128)(2,1)} %bitcast.53, bf16[32,128,256]{2,1,0:T(8,128)(2,1)S(1)} %bitcast.50, bf16[32,256,2048]{2,1,0:T(8,128)(2,1)} %bitcast.52), kind=kOutput, calls=%fused_computation.4 | convolution fusion | flops 4320133120 | bytes 69206016 | tf_op jit(solution)/shard_map/bsk,bkn->bsn/dot_general | solution.py:18
  99.3 8.4 %fusion.16 = f32[4096,256]{1,0:T(8,128)S(1)} fusion(bf16[4096,2048]{1,0:T(8,128)(2,1)} %bitcast.54, bf16[2048,256]{1,0:T(8,128)(2,1)S(1)} %copy-done.4), kind=kOutput, calls=%fused_computation.44 | convolution fusion | flops 4294967296 | bytes 22020096 | tf_op jit(solution)/shard_map/dot_general | solution.py:28
  107.7 2.0 copy-done.2
  109.7 7.6 %convolution_multiply_fusion = f32[256,256]{0,1:T(8,128)} fusion(f32[4096,256]{1,0:T(8,128)S(1)} %fusion.16), kind=kOutput, calls=%fused_computation.11 | convolution fusion | flops 3221291008 | bytes 4456448 | tf_op jit(solution)/shard_map/dot_general | solution.py:32
  117.4 0.0 all-reduce.5.cloned.1.call-update
  117.4 0.0 all-reduce.7.cloned.1.call-start
  117.5 103.1 %all-reduce.5.cloned.1.call-done = f32[256,256]{0,1:T(8,128)} async-done(((f32[256,256]{0,1:T(8,128)}), f32[256,256]{0,1:T(8,128)}) %all-reduce.5.cloned.1.call-update) | async-done | bytes 262160 | tf_op jit(solution)/shard_map/psum | solution.py:33
  220.5 0.0 all-reduce.7.cloned.1.call-update
  220.5 0.2 all-reduce.9.cloned.1.call-start
  220.8 13.2 %fusion.3 = f32[2048,256]{1,0:T(8,128)} fusion(bf16[4096,2048]{1,0:T(8,128)(2,1)} %bitcast.55, f32[4096,256]{1,0:T(8,128)} %copy-done.2), kind=kOutput, calls=%fused_computation.9 | convolution fusion | flops 4296015872 | bytes 23068672 | tf_op jit(solution)/shard_map/sn,sm->nm/dot_general | solution.py:38
  234.0 0.0 all-reduce.9.cloned.1.call-update
  234.0 28.1 %all-reduce.7.cloned.1.call-done = f32[256,256]{0,1:T(8,128)} async-done(((f32[256,256]{0,1:T(8,128)}), f32[256,256]{0,1:T(8,128)}) %all-reduce.7.cloned.1.call-update) | async-done | bytes 262160 | tf_op jit(solution)/shard_map/psum | solution.py:33
  262.1 1.1 copy.13
  263.2 1.0 fusion.5
  264.2 11.7 %cholesky.50 = f32[128,128]{1,0:T(8,128)S(1)} custom-call(f32[128,128]{1,0:T(8,128)S(1)} %cholesky.118), custom_call_target="Cholesky" | custom-call | tf_op jit(solution)/shard_map/jit(cholesky)/cholesky | solution.py:33
  275.9 9.8 %custom-call.16 = f32[1,128,128]{1,2,0:T(8,128)S(1)} custom-call(f32[1,128,128]{2,1,0:T(8,128)S(1)} %get-tuple-element.27), custom_call_target="InvertDiagBlocksLowerTriangular" | custom-call | tf_op jit(solution)/shard_map/jit(cholesky)/cholesky | solution.py:33
  285.8 0.2 constant_dynamic-update-slice_fusion.1
  286.0 0.3 convolution_subtract_fusion.1
  286.2 11.9 %cholesky.105 = f32[128,128]{1,0:T(8,128)S(1)} custom-call(f32[128,128]{1,0:T(8,128)S(1)} %convolution_subtract_fusion.1), custom_call_target="Cholesky" | custom-call | tf_op jit(solution)/shard_map/jit(cholesky)/cholesky | solution.py:33
  298.2 0.7 compare_reduce_fusion
  300.2 0.1 triangular_solve.73
  300.3 4.0 while.1
  300.3 0.6 fusion.31
  300.9 1.3 bitcast_dynamic-update-slice_fusion.2
  302.3 0.6 fusion.31
  302.9 1.3 bitcast_dynamic-update-slice_fusion.2
  304.3 19.7 %custom-call.17 = f32[2,128,128]{1,2,0:T(8,128)S(1)} custom-call(f32[2,128,128]{2,1,0:T(8,128)S(1)} %get-tuple-element.9), custom_call_target="InvertDiagBlocksLowerTriangular" | custom-call | tf_op jit(solution)/shard_map/triangular_solve | solution.py:34
  324.0 0.0 copy-start.3
  324.0 3.7 fusion.1
  327.7 3.6 convolution_subtract_fusion
  331.3 2.0 fusion.11
  333.3 2.4 pad_maximum_fusion
  335.7 5.6 %copy.14 = f32[4096,256]{1,0:T(8,128)} copy(f32[4096,256]{0,1:T(8,128)} %pad_maximum_fusion) | data formatting | bytes 8388608
  341.3 79.4 %all-reduce.9.cloned.1.call-done = f32[2048,256]{1,0:T(8,128)} async-done(((f32[2048,256]{1,0:T(8,128)}), f32[2048,256]{1,0:T(8,128)}) %all-reduce.9.cloned.1.call-update) | async-done | bytes 2097168 | tf_op jit(solution)/shard_map/psum | solution.py:39
  420.8 0.7 dynamic-slice_multiply_fusion
  421.5 0.2 fusion.9
  421.7 0.2 convolution_subtract_fusion.2
  421.9 0.2 fusion.10
  422.1 0.6 pad_maximum_fusion.1
  (17 shorter events, 0.2 us)
Async XLA Ops:
  7.2 68.7 %copy-start = (bf16[4096,256]{1,0:T(8,128)(2,1)S(1)}, bf16[4096,256]{1,0:T(8,128)(2,1)}, u32[]{:S(2)}) copy-start(bf16[4096,256]{1,0:T(8,128)(2,1)} %param.6) | copy-start | bytes 6291460
  7.2 53.8 %all-gather.2.cloned.1.call-start = ((), (), s32[]{:S(2)}) async-start(), calls=%async_computation | async-start | bytes 5242880 | tf_op jit(solution)/shard_map/all_gather | solution.py:12
  7.9 212.6 %all-reduce.5.cloned.1.call-start = ((), (), s32[]{:S(2)}) async-start(), calls=%async_computation.1 | async-start | bytes 524288 | tf_op jit(solution)/shard_map/psum | solution.py:33
  75.8 23.4 %copy-start.4 = (bf16[2048,256]{1,0:T(8,128)(2,1)S(1)}, bf16[2048,256]{1,0:T(8,128)(2,1)}, u32[]{:S(2)}) copy-start(bf16[2048,256]{1,0:T(8,128)(2,1)} %param.8) | copy-start | bytes 3145732
  107.7 2.0 copy-start.2
  117.4 144.7 %all-reduce.7.cloned.1.call-start = ((), (), s32[]{:S(2)}) async-start(), calls=%async_computation.2 | async-start | bytes 524288 | tf_op jit(solution)/shard_map/psum | solution.py:33
  220.5 200.2 %all-reduce.9.cloned.1.call-start = ((), (), s32[]{:S(2)}) async-start(), calls=%async_computation.3 | async-start | bytes 4194304 | tf_op jit(solution)/shard_map/psum | solution.py:39
  324.0 3.8 copy-start.3
  333.3 89.4 %copy-start.1 = (bf16[4096,256]{1,0:T(8,128)(2,1)S(1)}, bf16[4096,256]{1,0:T(8,128)(2,1)}, u32[]{:S(2)}) copy-start(bf16[4096,256]{1,0:T(8,128)(2,1)} %param.6) | copy-start | bytes 6291460
Sparse Core Ops, SparseCore 0:
  9.7 51.2 all-gather.1
  117.5 102.9 all-reduce.4
  222.9 39.1 all-reduce.6
  266.8 153.9 all-reduce.8
